TPU v7x, 32 devices: a whole 2x2x4 slice. The times are simulated.
32 devices in a mesh: samp: 2 (over core), grid: 16 (over z, y, x).
Axes of the slice: x: 2, y: 2, z: 4, core: 2. Of those that a mesh axis runs over, the one named last changes fastest.
Arguments:
- log_coef: float32 [2, 1024, 2048], P('samp', 'grid'), may hold values from -4 to 4
- source: float32 [2, 1024, 2048], P('samp', 'grid'), may hold values from -0.6 to 0.6
Outputs:
- correction: float32 [2, 1024, 2048], P('samp', 'grid')
- level_mean: float32 [1024, 2048], P('grid', 'samp')
- level_var: float32 [1024, 2048], P('grid', 'samp')
All inputs are finite; a program needn't handle non-finite values.
Results may differ from a plain program's by a relative error of at most 0.0003.
Values sent between devices are 32-bit elements; how exact they have to be, the bound alone decides.
A program may use at most 192 MiB of HBM per device.

v0:
```python
import jax
import jax.numpy as jnp
from jax import lax
from jax.sharding import PartitionSpec as P

LEVELS = 5
VCYCLES = 2
COARSE_SWEEPS = 4


damping = 0.8


def extended_2(value, sides, width):
    for axis, dim in sides:
        peers, length = (lax.axis_size(axis), value.shape[dim])
        up = [(i, (i + 1) % peers) for i in range(peers - 1)]
        down = [(j, i) for i, j in up]
        last = lax.slice_in_dim(value, length - width, length, axis=dim)
        initial = lax.slice_in_dim(value, 0, width, axis=dim)
        before = lax.ppermute(last, axis, up)
        after = lax.ppermute(initial, axis, down)
        value = jnp.concatenate([before, value, after], axis=dim)
    return value


def harmonic(former, latter):
    return 2.0 * former * latter / (former + latter)


def halve(coeffs):
    row_count, col_count = coeffs.shape
    return jnp.mean(coeffs.reshape(row_count // 2, 2, col_count // 2, 2), axis=(1, 3))


def quad_sum(values):
    row_count, col_count = values.shape
    return jnp.sum(values.reshape(row_count // 2, 2, col_count // 2, 2), axis=(1, 3))


def expand(values):
    return jnp.repeat(jnp.repeat(values, 2, axis=0), 2, axis=1)


def side_weights(coeffs):
    shifted = jnp.concatenate([coeffs[:, 1:], coeffs[:, -1:]], axis=1)
    east_face = harmonic(coeffs, shifted)
    west_face = jnp.concatenate([harmonic(coeffs[:, :1], coeffs[:, :1]), east_face[:, :-1]], axis=1)
    return (west_face, east_face)


def slab_weights(padded, coeffs, margin, is_top, is_bottom):
    col_count = coeffs.shape[1]
    upper = jnp.where(is_top, jnp.broadcast_to(coeffs[:1], (margin, col_count)), padded[:margin])
    lower = jnp.where(
        is_bottom, jnp.broadcast_to(coeffs[-1:], (margin, col_count)), padded[-margin:]
    )
    extended = jnp.concatenate([upper, coeffs, lower], axis=0)
    west_face, east_face = side_weights(extended)
    return (west_face, east_face, harmonic(extended[:-1], extended[1:]))


def band(weights, start, count):
    west_face, east_face, vertical = weights
    return (
        west_face[start : start + count],
        east_face[start : start + count],
        vertical[start - 1 : start + count],
    )


def pad_rows(values):
    return jnp.pad(values, ((1, 1), (0, 0)))


def apply_rows(wide, west_face, east_face, vertical):
    middle = wide[1:-1]
    zero_column = jnp.zeros_like(middle[:, :1])
    west_values = jnp.concatenate([zero_column, middle[:, :-1]], axis=1)
    east_values = jnp.concatenate([middle[:, 1:], zero_column], axis=1)
    north_face = vertical[:-1]
    south_face = vertical[1:]
    diagonal = west_face + east_face + north_face + south_face
    applied = diagonal * middle - (
        west_face * west_values
        + east_face * east_values
        + north_face * wide[:-2]
        + south_face * wide[2:]
    )
    return (middle, applied, diagonal)


def relax_rows(wide, right_side, west_face, east_face, vertical):
    middle, applied, diagonal = apply_rows(wide, west_face, east_face, vertical)
    return middle + damping * (right_side - applied) / diagonal


def pair_sweep(wide, side_wide, weights, row_count, is_top, is_bottom):
    first_pass = relax_rows(wide, side_wide[1:-1], *band(weights, 1, row_count + 2))
    position = lax.broadcasted_iota(jnp.int32, (row_count + 2, 1), 0)
    outside = jnp.logical_or(
        jnp.logical_and(position == 0, is_top),
        jnp.logical_and(position == row_count + 1, is_bottom),
    )
    first_pass = jnp.where(outside, jnp.float32(0.0), first_pass)
    return relax_rows(first_pass, side_wide[2:-2], *band(weights, 2, row_count))


def local(log_coef, source):
    depth = 2
    grid_count = lax.axis_size("grid")
    grid_index = lax.axis_index("grid")
    is_top = grid_index == 0
    is_bottom = grid_index == grid_count - 1
    coeffs = jnp.exp(log_coef[0])
    ladder = []
    margins = []
    for height in range(LEVELS):
        if height:
            coeffs = halve(coeffs)
        if height < LEVELS - 1:
            padded = extended_2(coeffs, (("grid", 0),), depth)
            ladder.append(slab_weights(padded, coeffs, depth, is_top, is_bottom))
            margins.append(depth)
        else:
            padded = extended_2(coeffs, (("grid", 0),), 1)
            ladder.append(slab_weights(padded, coeffs, 1, is_top, is_bottom))
            margins.append(1)

    def residual_of(height, iterate, right_side):
        wide = extended_2(iterate, (("grid", 0),), 1)
        middle, applied, diagonal = apply_rows(
            wide, *band(ladder[height], margins[height], iterate.shape[0])
        )
        return right_side - applied

    def bottom_solve(right_side):
        row_count = right_side.shape[0]
        weights = band(ladder[-1], 1, row_count)
        iterate = relax_rows(pad_rows(jnp.zeros_like(right_side)), right_side, *weights)
        for repeat in range(COARSE_SWEEPS - 1):
            wide = extended_2(iterate, (("grid", 0),), 1)
            iterate = relax_rows(wide, right_side, *weights)
        return iterate

    def vcycle_slab(height, iterate, right_side):
        if height == LEVELS - 1:
            return bottom_solve(right_side)
        row_count = iterate.shape[0]
        stacked = extended_2(jnp.stack((iterate, right_side)), (("grid", 1),), 2)
        side_wide = stacked[1]
        iterate = pair_sweep(stacked[0], side_wide, ladder[height], row_count, is_top, is_bottom)
        residual = residual_of(height, iterate, right_side)
        coarse_side = quad_sum(residual)
        errors = vcycle_slab(height + 1, jnp.zeros_like(coarse_side), coarse_side)
        iterate = iterate + expand(errors)
        wide = extended_2(iterate, (("grid", 0),), 2)
        iterate = pair_sweep(wide, side_wide, ladder[height], row_count, is_top, is_bottom)
        return iterate

    source_field = source[0]
    fine_field = jnp.zeros_like(source_field)
    for repeat in range(VCYCLES):
        fine_field = vcycle_slab(0, fine_field, source_field)
    coarse_side = quad_sum(source_field)
    coarse = jnp.zeros_like(coarse_side)
    for repeat in range(VCYCLES):
        coarse = vcycle_slab(1, coarse, coarse_side)
    correction = fine_field - expand(coarse)
    sample_total = lax.axis_size("samp")
    summed, squares = (
        lax.psum_scatter(correction, "samp", scatter_dimension=1, tiled=True),
        lax.psum_scatter(correction * correction, "samp", scatter_dimension=1, tiled=True),
    )
    level_mean = summed / sample_total
    level_var = (squares - sample_total * level_mean * level_mean) / (sample_total - 1)
    return (correction[None], level_mean, level_var)


def solution(mesh):
    in_specs = (P("samp", "grid", None), P("samp", "grid", None))
    out_specs = (P("samp", "grid", None), P("grid", "samp"), P("grid", "samp"))
    return jax.shard_map(local, mesh=mesh, in_specs=in_specs, out_specs=out_specs, check_vma=False)
```

profile of v0, /device:TPU:17, one launch (start us, length us, event | category | flops | bytes accessed | tf_op | source)
XLA Modules:
  0.0 1238.2 jit_solution(12206661710002608845)
XLA Ops:
  32.0 36.9 %exp.16 = f32[32,2,1024,2]{3,2,1,0:T(8,128)} reshape(f32[1,64,2048]{2,1,0:T(8,128)} %copy.385) | data formatting | bytes 1048576 | tf_op jit(solution)/shard_map/exp | solution.py:115
  68.9 13.2 %reduce_sum.172 = f32[32,1024]{1,0:T(8,128)S(1)} reduce(f32[32,2,1024,2]{3,2,1,0:T(8,128)} %exp.16, f32[]{:T(128)} %constant.16.clone.1), dimensions={1,3}, to_apply=%region_1.2 | reduce | flops 98304 | bytes 655364 | tf_op jit(solution)/shard_map/reduce_sum | solution.py:33
  82.1 9.8 div.308
  113.8 36.9 %reshape_squeeze.3 = f32[32,2,1024,2]{3,2,1,0:T(8,128)} reshape(f32[1,64,2048]{2,1,0:T(8,128)} %param.3) | data formatting | bytes 1048576 | tf_op jit(solution)/shard_map/reshape;squeeze | solution.py:38
  152.2 13.9 %reduce_sum.183 = f32[32,1024]{1,0:T(8,128)} reduce(f32[32,2,1024,2]{3,2,1,0:T(8,128)} %reshape_squeeze.3, f32[]{:T(128)} %constant.16.clone.1), dimensions={1,3}, to_apply=%region_12.13 | reduce | flops 98304 | bytes 655364 | tf_op jit(solution)/shard_map/reduce_sum | solution.py:38
  168.9 5.2 collective-permute-start.21
  247.6 6.2 fusion.42
  256.1 36.9 %reshape.303 = f32[32,2,1024,2]{3,2,1,0:T(8,128)} reshape(f32[64,2048]{1,0:T(8,128)} %copy.384) | data formatting | bytes 1048576 | tf_op jit(solution)/shard_map/reshape | solution.py:38
  293.0 13.2 %reduce_sum.171 = f32[32,1024]{1,0:T(8,128)S(1)} reduce(f32[32,2,1024,2]{3,2,1,0:T(8,128)} %reshape.303, f32[]{:T(128)} %constant.16.clone.1), dimensions={1,3}, to_apply=%region_0.1 | reduce | flops 98304 | bytes 655364 | tf_op jit(solution)/shard_map/reduce_sum | solution.py:38
  331.6 10.5 reshape.304
  401.8 5.2 collective-permute-start.27
  410.4 5.4 collective-permute-start.29
  432.1 5.4 collective-permute-start.33
  458.9 5.2 collective-permute-start.35
  578.4 6.2 fusion.11
  586.9 36.9 %reshape.315 = f32[32,2,1024,2]{3,2,1,0:T(8,128)} reshape(f32[64,2048]{1,0:T(8,128)} %copy.412) | data formatting | bytes 1048576 | tf_op jit(solution)/shard_map/reshape | solution.py:38
  623.8 13.9 %reduce_sum.179 = f32[32,1024]{1,0:T(8,128)} reduce(f32[32,2,1024,2]{3,2,1,0:T(8,128)} %reshape.315, f32[]{:T(128)} %constant.16.clone.1), dimensions={1,3}, to_apply=%region_8.9 | reduce | flops 98304 | bytes 655364 | tf_op jit(solution)/shard_map/reduce_sum | solution.py:38
  638.5 5.2 collective-permute-start.45
  665.2 10.5 reshape.316
  691.6 10.5 reshape.327
  802.1 5.2 collective-permute-start.57
  809.3 5.2 collective-permute-start.83
  817.3 5.2 collective-permute-start.59
  842.6 5.2 collective-permute-start.87
  940.9 5.2 collective-permute-start.93
  993.9 10.5 reshape.336
  1069.5 5.3 collective-permute-start.107
  1078.1 5.4 collective-permute-start.109
  1099.9 5.3 collective-permute-start.113
  1122.6 6.5 fusion.79
  1161.9 54.3 %reduce-scatter.5.cloned.1.call-done = f32[64,1024]{0,1:T(8,128)} async-done(((f32[64,2048]{0,1:T(8,128)}), f32[64,1024]{0,1:T(8,128)}) %reduce-scatter.5.cloned.1.call-update) | async-done | bytes 262160 | tf_op jit(solution)/shard_map/reduce_scatter | solution.py:173
  1216.2 11.9 reduce-scatter.3.cloned.1.call-done
  (947 shorter events, 808.1 us)
Async XLA Ops:
  7.2 1209.1 %reduce-scatter.5.cloned.1.call-start = ((), (), s32[]{:S(2)}) async-start(), calls=%async_computation.3 | async-start | bytes 1572864 | tf_op jit(solution)/shard_map/reduce_scatter | solution.py:173
  12.6 201.3 %collective-permute-start.1 = (f32[2,2,2048]{2,1,0:T(2,128)S(1)}, f32[2,2,2048]{2,1,0:T(2,128)S(1)}, u32[]{:S(2)}, u32[]{:S(2)}) collective-permute-start(f32[2,2,2048]{2,1,0:T(2,128)S(1)} %copy.369), channel_id=1, source_target_pairs={{1,0},{2,1},{3,2},{4,3},{5,4},{6,5},{7,6},{8,7},{9,8},{10,9},{11,1... | collective-permute-start | bytes 98312 | tf_op jit(solution)/shard_map/ppermute | solution.py:22
  17.8 198.1 %collective-permute-start = (f32[2,2,2048]{2,1,0:T(2,128)}, f32[2,2,2048]{2,1,0:T(2,128)}, u32[]{:S(2)}, u32[]{:S(2)}) collective-permute-start(f32[2,2,2048]{2,1,0:T(2,128)} %copy.368), channel_id=1, source_target_pairs={{0,1},{1,2},{2,3},{3,4},{4,5},{5,6},{6,7},{7,8},{8,9},{9,10},{10,1... | collective-permute-start | bytes 98312 | tf_op jit(solution)/shard_map/ppermute | solution.py:21
  25.7 180.1 %collective-permute-start.3 = (f32[2,2048]{1,0:T(2,128)}, f32[2,2048]{1,0:T(2,128)}, u32[]{:S(2)}, u32[]{:S(2)}) collective-permute-start(f32[2,2048]{1,0:T(2,128)} %copy.374), channel_id=1, source_target_pairs={{1,0},{2,1},{3,2},{4,3},{5,4},{6,5},{7,6},{8,7},{9,8},{10,9},{11,1... | collective-permute-start | bytes 49160 | tf_op jit(solution)/shard_map/ppermute | solution.py:22
  104.3 62.7 %collective-permute-start.25 = (f32[1,128]{1,0:T(1,128)S(1)}, f32[1,128]{1,0:T(1,128)S(1)}, u32[]{:S(2)}, u32[]{:S(2)}) collective-permute-start(f32[1,128]{1,0:T(1,128)S(1)} %get-tuple-element.378), channel_id=1, source_target_pairs={{1,0},{2,1},{3,2},{4,3},{5,4},{6,5},{7,6},{8,7},{9,8},{10,9},{11,1... | collective-permute-start | bytes 1544 | tf_op jit(solution)/shard_map/ppermute | solution.py:22
  106.3 62.7 %collective-permute-start.24 = (f32[1,128]{1,0:T(1,128)S(1)}, f32[1,128]{1,0:T(1,128)S(1)}, u32[]{:S(2)}, u32[]{:S(2)}) collective-permute-start(f32[1,128]{1,0:T(1,128)S(1)} %get-tuple-element.379), channel_id=1, source_target_pairs={{0,1},{1,2},{2,3},{3,4},{4,5},{5,6},{6,7},{7,8},{8,9},{9,10},{10,1... | collective-permute-start | bytes 1544 | tf_op jit(solution)/shard_map/ppermute | solution.py:21
  167.0 40.8 %collective-permute-start.2 = (f32[2,2048]{1,0:T(2,128)S(1)}, f32[2,2048]{1,0:T(2,128)S(1)}, u32[]{:S(2)}, u32[]{:S(2)}) collective-permute-start(f32[2,2048]{1,0:T(2,128)S(1)} %copy.373), channel_id=1, source_target_pairs={{0,1},{1,2},{2,3},{3,4},{4,5},{5,6},{6,7},{7,8},{8,9},{9,10},{10,1... | collective-permute-start | bytes 49160 | tf_op jit(solution)/shard_map/ppermute | solution.py:21
  432.1 17.4 %collective-permute-start.33 = (f32[2,256]{1,0:T(2,128)S(1)}, f32[2,256]{1,0:T(2,128)S(1)}, u32[]{:S(2)}, u32[]{:S(2)}) collective-permute-start(f32[2,256]{1,0:T(2,128)S(1)} %get-tuple-element.275), channel_id=1, source_target_pairs={{1,0},{2,1},{3,2},{4,3},{5,4},{6,5},{7,6},{8,7},{9,8},{10,9},{11,1... | collective-permute-start | bytes 6152 | tf_op jit(solution)/shard_map/ppermute | solution.py:22
  440.9 25.2 %collective-permute-start.71 = (f32[2,2,1024]{2,1,0:T(2,128)}, f32[2,2,1024]{2,1,0:T(2,128)}, u32[]{:S(2)}, u32[]{:S(2)}) collective-permute-start(f32[2,2,1024]{2,1,0:T(2,128)} %get-tuple-element.155), channel_id=1, source_target_pairs={{1,0},{2,1},{3,2},{4,3},{5,4},{6,5},{7,6},{8,7},{9,8},{10,9},{11,1... | collective-permute-start | bytes 49160 | tf_op jit(solution)/shard_map/ppermute | solution.py:22
  446.0 20.0 %collective-permute-start.70 = (f32[2,2,1024]{2,1,0:T(2,128)}, f32[2,2,1024]{2,1,0:T(2,128)}, u32[]{:S(2)}, u32[]{:S(2)}) collective-permute-start(f32[2,2,1024]{2,1,0:T(2,128)} %get-tuple-element.154), channel_id=1, source_target_pairs={{0,1},{1,2},{2,3},{3,4},{4,5},{5,6},{6,7},{7,8},{8,9},{9,10},{10,1... | collective-permute-start | bytes 49160 | tf_op jit(solution)/shard_map/ppermute | solution.py:21
  657.7 31.8 %collective-permute-start.73 = (f32[1,1024]{1,0:T(1,128)}, f32[1,1024]{1,0:T(1,128)}, u32[]{:S(2)}, u32[]{:S(2)}) collective-permute-start(f32[1,1024]{1,0:T(1,128)} %get-tuple-element.147), channel_id=1, source_target_pairs={{1,0},{2,1},{3,2},{4,3},{5,4},{6,5},{7,6},{8,7},{9,8},{10,9},{11,1... | collective-permute-start | bytes 12296 | tf_op jit(solution)/shard_map/ppermute | solution.py:22
  662.5 27.1 %collective-permute-start.72 = (f32[1,1024]{1,0:T(1,128)}, f32[1,1024]{1,0:T(1,128)}, u32[]{:S(2)}, u32[]{:S(2)}) collective-permute-start(f32[1,1024]{1,0:T(1,128)} %get-tuple-element.146), channel_id=1, source_target_pairs={{0,1},{1,2},{2,3},{3,4},{4,5},{5,6},{6,7},{7,8},{8,9},{9,10},{10,1... | collective-permute-start | bytes 12296 | tf_op jit(solution)/shard_map/ppermute | solution.py:21
  682.2 34.4 %collective-permute-start.49 = (f32[2,2,512]{2,1,0:T(2,128)}, f32[2,2,512]{2,1,0:T(2,128)}, u32[]{:S(2)}, u32[]{:S(2)}) collective-permute-start(f32[2,2,512]{2,1,0:T(2,128)} %get-tuple-element.201), channel_id=1, source_target_pairs={{1,0},{2,1},{3,2},{4,3},{5,4},{6,5},{7,6},{8,7},{9,8},{10,9},{11,1... | collective-permute-start | bytes 24584 | tf_op jit(solution)/shard_map/ppermute | solution.py:22
  687.4 29.3 %collective-permute-start.48 = (f32[2,2,512]{2,1,0:T(2,128)}, f32[2,2,512]{2,1,0:T(2,128)}, u32[]{:S(2)}, u32[]{:S(2)}) collective-permute-start(f32[2,2,512]{2,1,0:T(2,128)} %get-tuple-element.200), channel_id=1, source_target_pairs={{0,1},{1,2},{2,3},{3,4},{4,5},{5,6},{6,7},{7,8},{8,9},{9,10},{10,1... | collective-permute-start | bytes 24584 | tf_op jit(solution)/shard_map/ppermute | solution.py:21
  728.9 22.4 %collective-permute-start.77 = (f32[1,512]{1,0:T(1,128)}, f32[1,512]{1,0:T(1,128)}, u32[]{:S(2)}, u32[]{:S(2)}) collective-permute-start(f32[1,512]{1,0:T(1,128)} %get-tuple-element.221), channel_id=1, source_target_pairs={{1,0},{2,1},{3,2},{4,3},{5,4},{6,5},{7,6},{8,7},{9,8},{10,9},{11,1... | collective-permute-start | bytes 6152 | tf_op jit(solution)/shard_map/ppermute | solution.py:22
  733.5 17.8 %collective-permute-start.76 = (f32[1,512]{1,0:T(1,128)}, f32[1,512]{1,0:T(1,128)}, u32[]{:S(2)}, u32[]{:S(2)}) collective-permute-start(f32[1,512]{1,0:T(1,128)} %get-tuple-element.220), channel_id=1, source_target_pairs={{0,1},{1,2},{2,3},{3,4},{4,5},{5,6},{6,7},{7,8},{8,9},{9,10},{10,1... | collective-permute-start | bytes 6152 | tf_op jit(solution)/shard_map/ppermute | solution.py:21
  744.2 24.7 %collective-permute-start.53 = (f32[2,2,256]{2,1,0:T(2,128)}, f32[2,2,256]{2,1,0:T(2,128)}, u32[]{:S(2)}, u32[]{:S(2)}) collective-permute-start(f32[2,2,256]{2,1,0:T(2,128)} %get-tuple-element.273), channel_id=1, source_target_pairs={{1,0},{2,1},{3,2},{4,3},{5,4},{6,5},{7,6},{8,7},{9,8},{10,9},{11,1... | collective-permute-start | bytes 12296 | tf_op jit(solution)/shard_map/ppermute | solution.py:22
  749.4 19.6 %collective-permute-start.52 = (f32[2,2,256]{2,1,0:T(2,128)}, f32[2,2,256]{2,1,0:T(2,128)}, u32[]{:S(2)}, u32[]{:S(2)}) collective-permute-start(f32[2,2,256]{2,1,0:T(2,128)} %get-tuple-element.272), channel_id=1, source_target_pairs={{0,1},{1,2},{2,3},{3,4},{4,5},{5,6},{6,7},{7,8},{8,9},{9,10},{10,1... | collective-permute-start | bytes 12296 | tf_op jit(solution)/shard_map/ppermute | solution.py:21
  831.5 16.3 %collective-permute-start.60 = (f32[1,128]{1,0:T(1,128)S(1)}, f32[1,128]{1,0:T(1,128)S(1)}, u32[]{:S(2)}, u32[]{:S(2)}) collective-permute-start(f32[1,128]{1,0:T(1,128)S(1)} %get-tuple-element.308), channel_id=1, source_target_pairs={{0,1},{1,2},{2,3},{3,4},{4,5},{5,6},{6,7},{7,8},{8,9},{9,10},{10,1... | collective-permute-start | bytes 1544 | tf_op jit(solution)/shard_map/ppermute | solution.py:21
  840.7 20.3 %collective-permute-start.86 = (f32[1,128]{1,0:T(1,128)}, f32[1,128]{1,0:T(1,128)}, u32[]{:S(2)}, u32[]{:S(2)}) collective-permute-start(f32[1,128]{1,0:T(1,128)} %get-tuple-element.362), channel_id=1, source_target_pairs={{0,1},{1,2},{2,3},{3,4},{4,5},{5,6},{6,7},{7,8},{8,9},{9,10},{10,1... | collective-permute-start | bytes 1544 | tf_op jit(solution)/shard_map/ppermute | solution.py:21
  842.6 18.4 %collective-permute-start.87 = (f32[1,128]{1,0:T(1,128)}, f32[1,128]{1,0:T(1,128)}, u32[]{:S(2)}, u32[]{:S(2)}) collective-permute-start(f32[1,128]{1,0:T(1,128)} %get-tuple-element.363), channel_id=1, source_target_pairs={{1,0},{2,1},{3,2},{4,3},{5,4},{6,5},{7,6},{8,7},{9,8},{10,9},{11,1... | collective-permute-start | bytes 1544 | tf_op jit(solution)/shard_map/ppermute | solution.py:22
  855.7 18.4 %collective-permute-start.63 = (f32[2,256]{1,0:T(2,128)}, f32[2,256]{1,0:T(2,128)}, u32[]{:S(2)}, u32[]{:S(2)}) collective-permute-start(f32[2,256]{1,0:T(2,128)} %get-tuple-element.267), channel_id=1, source_target_pairs={{1,0},{2,1},{3,2},{4,3},{5,4},{6,5},{7,6},{8,7},{9,8},{10,9},{11,1... | collective-permute-start | bytes 6152 | tf_op jit(solution)/shard_map/ppermute | solution.py:22
  857.6 16.5 %collective-permute-start.62 = (f32[2,256]{1,0:T(2,128)}, f32[2,256]{1,0:T(2,128)}, u32[]{:S(2)}, u32[]{:S(2)}) collective-permute-start(f32[2,256]{1,0:T(2,128)} %get-tuple-element.266), channel_id=1, source_target_pairs={{0,1},{1,2},{2,3},{3,4},{4,5},{5,6},{6,7},{7,8},{8,9},{9,10},{10,1... | collective-permute-start | bytes 6152 | tf_op jit(solution)/shard_map/ppermute | solution.py:21
  889.4 20.4 %collective-permute-start.65 = (f32[2,512]{1,0:T(2,128)}, f32[2,512]{1,0:T(2,128)}, u32[]{:S(2)}, u32[]{:S(2)}) collective-permute-start(f32[2,512]{1,0:T(2,128)} %get-tuple-element.195), channel_id=1, source_target_pairs={{1,0},{2,1},{3,2},{4,3},{5,4},{6,5},{7,6},{8,7},{9,8},{10,9},{11,1... | collective-permute-start | bytes 12296 | tf_op jit(solution)/shard_map/ppermute | solution.py:22
  892.1 17.7 %collective-permute-start.64 = (f32[2,512]{1,0:T(2,128)}, f32[2,512]{1,0:T(2,128)}, u32[]{:S(2)}, u32[]{:S(2)}) collective-permute-start(f32[2,512]{1,0:T(2,128)} %get-tuple-element.194), channel_id=1, source_target_pairs={{0,1},{1,2},{2,3},{3,4},{4,5},{5,6},{6,7},{7,8},{8,9},{9,10},{10,1... | collective-permute-start | bytes 12296 | tf_op jit(solution)/shard_map/ppermute | solution.py:21
  926.2 21.9 %collective-permute-start.67 = (f32[2,1024]{1,0:T(2,128)}, f32[2,1024]{1,0:T(2,128)}, u32[]{:S(2)}, u32[]{:S(2)}) collective-permute-start(f32[2,1024]{1,0:T(2,128)} %get-tuple-element.119), channel_id=1, source_target_pairs={{1,0},{2,1},{3,2},{4,3},{5,4},{6,5},{7,6},{8,7},{9,8},{10,9},{11,1... | collective-permute-start | bytes 24584 | tf_op jit(solution)/shard_map/ppermute | solution.py:22
  929.5 18.6 %collective-permute-start.66 = (f32[2,1024]{1,0:T(2,128)}, f32[2,1024]{1,0:T(2,128)}, u32[]{:S(2)}, u32[]{:S(2)}) collective-permute-start(f32[2,1024]{1,0:T(2,128)} %get-tuple-element.118), channel_id=1, source_target_pairs={{0,1},{1,2},{2,3},{3,4},{4,5},{5,6},{6,7},{7,8},{8,9},{9,10},{10,1... | collective-permute-start | bytes 24584 | tf_op jit(solution)/shard_map/ppermute | solution.py:21
  953.8 25.2 %collective-permute-start.95 = (f32[2,2,1024]{2,1,0:T(2,128)}, f32[2,2,1024]{2,1,0:T(2,128)}, u32[]{:S(2)}, u32[]{:S(2)}) collective-permute-start(f32[2,2,1024]{2,1,0:T(2,128)} %get-tuple-element.83), channel_id=1, source_target_pairs={{1,0},{2,1},{3,2},{4,3},{5,4},{6,5},{7,6},{8,7},{9,8},{10,9},{11,1... | collective-permute-start | bytes 49160 | tf_op jit(solution)/shard_map/ppermute | solution.py:22
  957.6 21.3 %collective-permute-start.94 = (f32[2,2,1024]{2,1,0:T(2,128)}, f32[2,2,1024]{2,1,0:T(2,128)}, u32[]{:S(2)}, u32[]{:S(2)}) collective-permute-start(f32[2,2,1024]{2,1,0:T(2,128)} %get-tuple-element.82), channel_id=1, source_target_pairs={{0,1},{1,2},{2,3},{3,4},{4,5},{5,6},{6,7},{7,8},{8,9},{9,10},{10,1... | collective-permute-start | bytes 49160 | tf_op jit(solution)/shard_map/ppermute | solution.py:21
  969.6 46.6 %collective-permute-start.69 = (f32[2,2048]{1,0:T(2,128)}, f32[2,2048]{1,0:T(2,128)}, u32[]{:S(2)}, u32[]{:S(2)}) collective-permute-start(f32[2,2048]{1,0:T(2,128)} %copy.421), channel_id=1, source_target_pairs={{1,0},{2,1},{3,2},{4,3},{5,4},{6,5},{7,6},{8,7},{9,8},{10,9},{11,1... | collective-permute-start | bytes 49160 | tf_op jit(solution)/shard_map/ppermute | solution.py:22
  976.9 41.5 %collective-permute-start.68 = (f32[2,2048]{1,0:T(2,128)}, f32[2,2048]{1,0:T(2,128)}, u32[]{:S(2)}, u32[]{:S(2)}) collective-permute-start(f32[2,2048]{1,0:T(2,128)} %copy.420), channel_id=1, source_target_pairs={{0,1},{1,2},{2,3},{3,4},{4,5},{5,6},{6,7},{7,8},{8,9},{9,10},{10,1... | collective-permute-start | bytes 49160 | tf_op jit(solution)/shard_map/ppermute | solution.py:21
  1159.6 68.5 %reduce-scatter.3.cloned.1.call-start = ((), (), s32[]{:S(2)}) async-start(), calls=%async_computation.2 | async-start | bytes 1572864 | tf_op jit(solution)/shard_map/reduce_scatter | solution.py:172
  (208 other events, 1753.9 us)
Sparse Core Ops, SparseCore 0:
  1159.7 56.4 reduce-scatter.4
  1218.5 9.6 reduce-scatter.2
where the time goes:
time: 1260 us; the launch traced here: 1240 us
  local copies, waits for them, and re-layouts  475 us (38%)
  starting transfers between devices  377 us (30%)
  other arithmetic  242 us (19%)
  waiting for transfers between devices  128 us (10%)
  between operations  17.9 us (1%)
    ppermute x59, starting transfers between devices, extended_2(): after = lax.ppermute(initial, axis, down)  242 us
    reshape x14, local copies, waits for them, and re-layouts, quad_sum(): values.reshape(row_count // 2, 2, col_count // 2, 2)  140 us
    ppermute x59, starting transfers between devices, extended_2(): before = lax.ppermute(last, axis, up)  134 us
    reduce_sum x15, other arithmetic, quad_sum(): jnp.sum(values.reshape(row_count // 2, 2, col_count // 2, 2), axis=(1, 3))  78.2 us
    reshape x38, local copies, waits for them, and re-layouts, expand(): return jnp.repeat(jnp.repeat(values, 2, axis=0), 2, axis=1)  57.3 us
    ppermute x59, waiting for transfers between devices, extended_2(): before = lax.ppermute(last, axis, up)  56.8 us
    reduce_scatter x1, waiting for transfers between devices, local(): lax.psum_scatter(correction * correction, 'samp', scatter_dimension=1, ti...  54.3 us
    exp x3, local copies, waits for them, and re-layouts, local(): coeffs = jnp.exp(log_coef[0])  39.1 us
  transfers between devices with their start and end apart: 120, of which 31 were waited for; matrix products, arithmetic and copies ran while one was open for 30% of the time, Pallas kernels for 0%

commit v1 on v0

v1 whole, which is shorter than its diff:
```python
import functools

import jax
import jax.numpy as jnp
from jax import lax
from jax.experimental import pallas as pl
from jax.experimental.pallas import tpu as pltpu
from jax.sharding import PartitionSpec as P

CYCLES = 2
SUB = 8
LANE = 128
HALO = (8, 4, 6, 16, 8)
SHIFT = (None, 1, 2, 4, 0)
F32 = jnp.float32


def harmonic(a, b):
    return 2.0 * a * b / (a + b)


def iota(shape, axis):
    return lax.broadcasted_iota(jnp.int32, shape, axis)


def roll(x, shift, axis):
    return pltpu.roll(x, shift % x.shape[axis], axis)


def q_next(x):
    ax = x.ndim - 1
    return jnp.where(iota(x.shape, ax) < 112, roll(x, -16, ax), roll(x, -17, ax))


def q_prev(x):
    ax = x.ndim - 1
    return jnp.where(iota(x.shape, ax) >= 16, roll(x, 16, ax), roll(x, 17, ax))


def east_of(x, k):
    if k == 0:
        return q_next(x)
    ax = x.ndim - 2
    y = roll(x, -k, ax)
    return jnp.where(iota(x.shape, ax) < SUB - k, y, q_next(y))


def west_of(x, k):
    if k == 0:
        return q_prev(x)
    ax = x.ndim - 2
    y = roll(x, k, ax)
    return jnp.where(iota(x.shape, ax) >= k, y, q_prev(y))


def west_edge(shape, k):
    edge = iota(shape, len(shape) - 1) == 0
    if k:
        edge = jnp.logical_and(edge, iota(shape, len(shape) - 2) < k)
    return edge


def east_edge(shape, k):
    edge = iota(shape, len(shape) - 1) == LANE - 1
    if k:
        edge = jnp.logical_and(edge, iota(shape, len(shape) - 2) >= SUB - k)
    return edge


def pair_sum(x, k):
    ax = x.ndim - 2
    if 2 * k == SUB:
        return x + roll(x, k, ax)
    odd = (iota(x.shape, ax) // k) % 2 == 1
    return x + jnp.where(odd, roll(x, k, ax), roll(x, -k, ax))


def swap_bits(tiles, axis, count):
    tiles = list(tiles)
    for k in range(count):
        w = 1 << k
        bit = (iota(tiles[0].shape, axis) // w) % 2 == 1
        for t in range(len(tiles)):
            if t & w == 0:
                a, b = tiles[t], tiles[t | w]
                tiles[t] = jnp.where(bit, roll(b, w, axis), a)
                tiles[t | w] = jnp.where(bit, b, roll(a, -w, axis))
    return tiles


def blocks(lo, hi, size, body):
    count = (hi - lo) // size
    if count > 1:
        lax.fori_loop(0, count, lambda j, c: (body(lo + j * size, size), c)[1], 0)
    elif count == 1:
        body(lo, size)
    rest = (hi - lo) - count * size
    if rest:
        body(lo + count * size, rest)


def kernel(grid_count, own, lc_hbm, src_hbm, corr, mean, var, rawc, raws, b0, c0, v0a, v0b, nf0, w0, m0, e0, d0,
           di0, lev, rc2, rc3, rb2, rv1, rb3, rv0, rv1c, rcorr, send_sem, recv_sem, load_sem):
    me = lax.axis_index("grid")
    samp = lax.axis_index("samp")
    n0 = own[0]
    counter = [0]

    def to_grid(dist, src, dst):
        k = counter[0]
        counter[0] += 1
        target = me + dist
        copy = pltpu.make_async_remote_copy(
            src_ref=src, dst_ref=dst, send_sem=send_sem.at[k], recv_sem=recv_sem.at[k],
            device_id={"grid": target}, device_id_type=pl.DeviceIdType.MESH)
        sends = target >= 0 if dist < 0 else target < grid_count
        source = me - dist
        gets = source < grid_count if dist < 0 else source >= 0
        return copy, sends, gets

    def start(items):
        for copy, sends, gets in items:
            @pl.when(sends)
            def _():
                copy.start()

    def finish(items):
        for copy, sends, gets in items:
            @pl.when(sends)
            def _():
                copy.wait_send()

            @pl.when(gets)
            def _():
                copy.wait_recv()

    h0 = HALO[0]
    load_c = pltpu.make_async_copy(lc_hbm.at[0], rawc.at[pl.ds(h0, n0)], load_sem.at[0])
    load_s = pltpu.make_async_copy(src_hbm.at[0], raws.at[pl.ds(h0, n0)], load_sem.at[1])
    load_c.start()
    load_s.start()

    edge = 2
    @pl.when(jnp.logical_or(me < edge, me >= grid_count - edge))
    def _():
        @pl.when(me == 0)
        def _():
            rawc[pl.ds(0, h0)] = jnp.zeros((h0, rawc.shape[1]), F32)
            raws[pl.ds(0, h0)] = jnp.zeros((h0, rawc.shape[1]), F32)

        @pl.when(me == grid_count - 1)
        def _():
            rawc[pl.ds(h0 + n0, h0)] = jnp.zeros((h0, rawc.shape[1]), F32)
            raws[pl.ds(h0 + n0, h0)] = jnp.zeros((h0, rawc.shape[1]), F32)

        rc2[...] = jnp.ones_like(rc2)
        rc3[...] = jnp.ones_like(rc3)
        for ref in (rb2, rv1, rb3, rv0, rv1c):
            for i in range(ref.shape[0]):
                ref[i] = jnp.zeros(ref.shape[1:], F32)

    barrier = pltpu.get_barrier_semaphore()
    for dist in (-2, -1, 1, 2):
        inside = me + dist >= 0 if dist < 0 else me + dist < grid_count

        @pl.when(inside)
        def _():
            pl.semaphore_signal(barrier, inc=1, device_id={"grid": me + dist}, device_id_type=pl.DeviceIdType.MESH)
    pl.semaphore_signal(barrier, inc=1, device_id={"samp": 1 - samp}, device_id_type=pl.DeviceIdType.MESH)
    below = jnp.minimum(me, 2)
    above = jnp.minimum(grid_count - 1 - me, 2)
    pl.semaphore_wait(barrier, 1 + below + above)

    raw_items = []
    for hbm, raw in ((lc_hbm, rawc), (src_hbm, raws)):
        raw_items.append(to_grid(-1, hbm.at[0, pl.ds(0, h0)], raw.at[pl.ds(h0 + n0, h0)]))
        raw_items.append(to_grid(1, hbm.at[0, pl.ds(n0 - h0, h0)], raw.at[pl.ds(0, h0)]))
    start(raw_items)

    tiles = rawc.shape[1] // LANE
    lane_bits = tiles.bit_length() - 1

    def load_group(raw, out, fn, g):
        base = pl.multiple_of(g * SUB, SUB)
        y = swap_bits([raw[pl.ds(base, SUB), t * LANE:(t + 1) * LANE] for t in range(tiles)], 1, lane_bits)
        for p in range(2):
            z = swap_bits(y[p::2], 0, 3)
            for r in range(SUB):
                out[base + r, p] = fn(z[r])

    def groups(raw, out, fn, lo, hi):
        lax.fori_loop(lo, hi, lambda g, c: (load_group(raw, out, fn, g), c)[1], 0)

    gh, gn = h0 // SUB, n0 // SUB
    load_c.wait()
    groups(rawc, c0, jnp.exp, gh, gh + gn)

    def children(level, j):
        return 2 * (j - HALO[level]) + HALO[level - 1]

    def coarse_coef(level, lo, hi):
        c = lev[level]["c"]

        def body(j, size):
            first = children(level, j)
            if level == 1:
                x = c0[pl.ds(first, 2 * size)].reshape(size, 4, SUB, LANE)
                c[pl.ds(j, size)] = 0.25 * (x[:, 0] + x[:, 1] + x[:, 2] + x[:, 3])
            else:
                x = lev[level - 1]["c"][pl.ds(first, 2 * size)].reshape(size, 2, SUB, LANE)
                c[pl.ds(j, size)] = 0.25 * pair_sum(x[:, 0] + x[:, 1], SHIFT[level - 1])
        blocks(lo, hi, 4, body)

    H = HALO
    for level in (1, 2, 3):
        coarse_coef(level, H[level], H[level] + own[level])
    c2, c3 = lev[2]["c"], lev[3]["c"]
    coef_items = [
        to_grid(-1, c2.at[pl.ds(H[2], H[2])], rc2.at[1]),
        to_grid(1, c2.at[pl.ds(H[2] + own[2] - H[2], H[2])], rc2.at[0]),
        to_grid(-1, c3.at[pl.ds(H[3], own[3])], rc3.at[2]),
        to_grid(-2, c3.at[pl.ds(H[3], own[3])], rc3.at[3]),
        to_grid(1, c3.at[pl.ds(H[3], own[3])], rc3.at[1]),
        to_grid(2, c3.at[pl.ds(H[3], own[3])], rc3.at[0]),
    ]
    start(coef_items)
    load_s.wait()
    groups(raws, b0, lambda x: x, gh, gh + gn)
    finish(raw_items)
    for raw, out, fn in ((rawc, c0, jnp.exp), (raws, b0, lambda x: x)):
        groups(raw, out, fn, 0, gh)
        groups(raw, out, fn, gh + gn, gh + gn + gh)
    coarse_coef(1, 0, H[1])
    coarse_coef(1, H[1] + own[1], 2 * H[1] + own[1])

    def row_mask(level, i, size, value):
        return iota((size, SUB, LANE), 0) + i == value

    def first_row(level):
        return H[level] - me * own[level]

    def end_row(level):
        return H[level] + (grid_count - me) * own[level]

    def inside_rows(level, i, size):
        at = iota((size, SUB, LANE), 0) + i
        return jnp.logical_and(at >= first_row(level), at < end_row(level))

    def vertical(level, c, out, lo, hi):
        def body(i, size):
            a, b = c(i - 1, size), c(i, size)
            top = row_mask(level, i, size, first_row(level))
            bottom = row_mask(level, i, size, end_row(level))
            out(i, size, harmonic(jnp.where(top, b, a), jnp.where(bottom, a, b)))
        blocks(lo, hi, 4, body)

    total0 = n0 + 2 * h0
    for p in range(2):
        def put(i, size, x):
            nf0[pl.ds(i, size), p] = x
        vertical(0, lambda i, size: c0[pl.ds(i, size), p], put, 1, total0)

    def weights0(i, size):
        a, b = c0[pl.ds(i, size), 0], c0[pl.ds(i, size), 1]
        we, ee = west_edge(a.shape, 1), east_edge(a.shape, 1)
        wf = harmonic(jnp.where(we, a, west_of(b, 1)), a)
        mf = harmonic(a, b)
        ef = harmonic(b, jnp.where(ee, b, east_of(a, 1)))
        w0[pl.ds(i, size)] = jnp.where(we, 0.0, wf)
        m0[pl.ds(i, size)] = mf
        e0[pl.ds(i, size)] = jnp.where(ee, 0.0, ef)
        inside = inside_rows(0, i, size)
        for p, (x, y) in enumerate(((wf, mf), (mf, ef))):
            d = x + y + nf0[pl.ds(i, size), p] + nf0[pl.ds(i + 1, size), p]
            d0[pl.ds(i, size), p] = d
            di0[pl.ds(i, size), p] = jnp.where(inside, 0.8 / d, 0.0)
    blocks(1, total0 - 1, 2, weights0)

    def coarse_weights(level):
        L = lev[level]
        k = SHIFT[level]
        total = own[level] + 2 * H[level]

        def put(i, size, x):
            L["nf"][pl.ds(i, size)] = x
        vertical(level, lambda i, size: L["c"][pl.ds(i, size)], put, 1, total)

        def body(i, size):
            c = L["c"][pl.ds(i, size)]
            we, ee = west_edge(c.shape, k), east_edge(c.shape, k)
            wf = harmonic(jnp.where(we, c, west_of(c, k)), c)
            ef = harmonic(c, jnp.where(ee, c, east_of(c, k)))
            L["w"][pl.ds(i, size)] = jnp.where(we, 0.0, wf)
            L["e"][pl.ds(i, size)] = jnp.where(ee, 0.0, ef)
            d = wf + ef + L["nf"][pl.ds(i, size)] + L["nf"][pl.ds(i + 1, size)]
            L["d"][pl.ds(i, size)] = d
            L["di"][pl.ds(i, size)] = jnp.where(inside_rows(level, i, size), 0.8 / d, 0.0)
        blocks(1, total - 1, 2, body)

    coarse_weights(1)

    def around0(v, i, size):
        sums = []
        u = [v[pl.ds(i, size), p] for p in range(2)]
        mid = m0[pl.ds(i, size)]
        sums.append(w0[pl.ds(i, size)] * west_of(u[1], 1) + mid * u[1])
        sums.append(mid * u[0] + e0[pl.ds(i, size)] * east_of(u[0], 1))
        for p in range(2):
            sums[p] = sums[p] + (nf0[pl.ds(i, size), p] * v[pl.ds(i - 1, size), p]
                                 + nf0[pl.ds(i + 1, size), p] * v[pl.ds(i + 1, size), p])
        return u, sums

    def sweep0(src, dst, halo):
        def body(i, size):
            u, sums = around0(src, i, size)
            for p in range(2):
                dst[pl.ds(i, size), p] = 0.2 * u[p] + di0[pl.ds(i, size), p] * (b0[pl.ds(i, size), p] + sums[p])
        blocks(h0 - halo, h0 + n0 + halo, 2, body)

    def restrict0(v, out, halo):
        def body(j, size):
            i = children(1, j)
            u, sums = around0(v, i, 2 * size)
            r = 0.0
            for p in range(2):
                r = r + (b0[pl.ds(i, 2 * size), p] - d0[pl.ds(i, 2 * size), p] * u[p] + sums[p])
            r = r.reshape(size, 2, SUB, LANE)
            out[0, pl.ds(j, size)] = r[:, 0] + r[:, 1]
        blocks(H[1] - halo, H[1] + own[1] + halo, 1, body)

    def around(level, v, pr, i, size):
        L = lev[level]
        k = SHIFT[level]
        u = v[pr, pl.ds(i, size)]
        s = (L["w"][pl.ds(i, size)] * west_of(u, k) + L["e"][pl.ds(i, size)] * east_of(u, k)
             + L["nf"][pl.ds(i, size)] * v[pr, pl.ds(i - 1, size)]
             + L["nf"][pl.ds(i + 1, size)] * v[pr, pl.ds(i + 1, size)])
        return u, s

    def sweep(level, src, dst, halo):
        L = lev[level]

        def body(i, size):
            for pr in range(2):
                u, s = around(level, src, pr, i, size)
                dst[pr, pl.ds(i, size)] = 0.2 * u + L["di"][pl.ds(i, size)] * (L["b"][pr, pl.ds(i, size)] + s)
        blocks(H[level] - halo, H[level] + own[level] + halo, 2, body)

    def first_sweep(level, dst, halo):
        L = lev[level]

        def body(i, size):
            for pr in range(2):
                dst[pr, pl.ds(i, size)] = L["di"][pl.ds(i, size)] * L["b"][pr, pl.ds(i, size)]
        blocks(H[level] - halo, H[level] + own[level] + halo, 4, body)

    def restrict(level, v, halo):
        L = lev[level]

        def body(j, size):
            i = children(level + 1, j)
            for pr in range(2):
                u, s = around(level, v, pr, i, 2 * size)
                r = L["b"][pr, pl.ds(i, 2 * size)] - L["d"][pl.ds(i, 2 * size)] * u + s
                r = r.reshape(size, 2, SUB, LANE)
                lev[level + 1]["b"][pr, pl.ds(j, size)] = pair_sum(r[:, 0] + r[:, 1], SHIFT[level])
        n = level + 1
        blocks(H[n] - halo, H[n] + own[n] + halo, 1, body)

    def correct(level, v, e, halo):
        n = level + 1

        def body(j, size):
            i = children(n, j)
            for pr in range(2):
                x = e[pr, pl.ds(j, size)]
                for r in range(2):
                    for q in range(size):
                        v[pr, i + 2 * q + r] = v[pr, i + 2 * q + r] + x[q]
        blocks(H[n] - halo, H[n] + own[n] + halo, 2, body)

    b1 = lev[1]["b"]

    def restrict_source(j, size):
        x = b0[pl.ds(children(1, j), 2 * size)].reshape(size, 4, SUB, LANE)
        b1[1, pl.ds(j, size)] = x[:, 0] + x[:, 1] + x[:, 2] + x[:, 3]
    blocks(0, own[1] + 2 * H[1], 2, restrict_source)

    for cycle in range(CYCLES):
        v1a, v1b = lev[1]["va"], lev[1]["vb"]
        if cycle == 0:
            def first0(i, size):
                for p in range(2):
                    v0b[pl.ds(i, size), p] = di0[pl.ds(i, size), p] * b0[pl.ds(i, size), p]
            blocks(h0 - 7, h0 + n0 + 7, 2, first0)
        else:
            sweep0(v0a, v0b, 7)
        sweep0(v0b, v0a, 6)
        restrict0(v0a, b1, 2)
        if cycle == 0:
            first_sweep(1, v1b, 3)
        else:
            def clear(i, size):
                v1a[0, pl.ds(i, size)] = jnp.zeros((size, SUB, LANE), F32)
            blocks(0, own[1] + 2 * H[1], 4, clear)
            sweep(1, v1a, v1b, 3)
        sweep(1, v1b, v1a, 2)
        restrict(1, v1a, 0)
        b2 = lev[2]["b"]
        items = [
            to_grid(-1, b2.at[:, pl.ds(H[2], 5)], rb2.at[cycle, 1]),
            to_grid(1, b2.at[:, pl.ds(H[2] + own[2] - 5, 5)], rb2.at[cycle, 0]),
            to_grid(-1, v1a.at[:, pl.ds(H[1], 3)], rv1.at[cycle, 1]),
            to_grid(1, v1a.at[:, pl.ds(H[1] + own[1] - 3, 3)], rv1.at[cycle, 0]),
        ]
        start(items)
        if cycle == 0:
            finish(coef_items)
            c2[pl.ds(0, H[2])] = rc2[0]
            c2[pl.ds(H[2] + own[2], H[2])] = rc2[1]
            for s in range(4):
                at = (0, own[3], H[3] + own[3], H[3] + 2 * own[3])[s]
                c3[pl.ds(at, own[3])] = rc3[s]
            coarse_coef(4, 0, own[4] + 2 * H[4])
            for level in (2, 3, 4):
                coarse_weights(level)
        finish(items)
        for pr in range(2):
            b2[pr, pl.ds(H[2] - 5, 5)] = rb2[cycle, 0, pr]
            b2[pr, pl.ds(H[2] + own[2], 5)] = rb2[cycle, 1, pr]
            v1a[pr, pl.ds(H[1] - 3, 3)] = rv1[cycle, 0, pr]
            v1a[pr, pl.ds(H[1] + own[1], 3)] = rv1[cycle, 1, pr]
        v2a, v2b = lev[2]["va"], lev[2]["vb"]
        first_sweep(2, v2b, 5)
        sweep(2, v2b, v2a, 4)
        restrict(2, v2a, 0)
        b3 = lev[3]["b"]
        mine = b3.at[:, pl.ds(H[3], own[3])]
        items = [
            to_grid(-1, mine, rb3.at[cycle, 2]),
            to_grid(-2, mine, rb3.at[cycle, 3]),
            to_grid(1, mine, rb3.at[cycle, 1]),
            to_grid(2, mine, rb3.at[cycle, 0]),
        ]
        start(items)
        finish(items)
        for s in range(4):
            at = (0, own[3], H[3] + own[3], H[3] + 2 * own[3])[s]
            for pr in range(2):
                b3[pr, pl.ds(at, own[3])] = rb3[cycle, s, pr]
        v3a, v3b = lev[3]["va"], lev[3]["vb"]
        v4a, v4b = lev[4]["va"], lev[4]["vb"]
        first_sweep(3, v3b, 13)
        sweep(3, v3b, v3a, 12)
        restrict(3, v3a, 5)
        first_sweep(4, v4b, 5)
        sweep(4, v4b, v4a, 4)
        sweep(4, v4a, v4b, 3)
        sweep(4, v4b, v4a, 2)
        correct(3, v3a, v4a, 2)
        sweep(3, v3a, v3b, 3)
        sweep(3, v3b, v3a, 2)
        correct(2, v2a, v3a, 2)
        sweep(2, v2a, v2b, 3)
        sweep(2, v2b, v2a, 2)
        correct(1, v1a, v2a, 2)
        sweep(1, v1a, v1b, 2)
        sweep(1, v1b, v1a, 1)

        def correct0(j, size):
            i = children(1, j)
            x = v1a[0, pl.ds(j, size)]
            for q in range(size):
                for r in range(2):
                    for p in range(2):
                        v0a[i + 2 * q + r, p] = v0a[i + 2 * q + r, p] + x[q]
        blocks(H[1] - 1, H[1] + own[1] + 1, 2, correct0)
        sweep0(v0a, v0b, 1)
        sweep0(v0b, v0a, 0)
        if cycle < CYCLES - 1:
            h1 = H[1]
            items = [
                to_grid(-1, v0a.at[pl.ds(h0, h0)], rv0.at[1]),
                to_grid(1, v0a.at[pl.ds(n0, h0)], rv0.at[0]),
                to_grid(-1, v1a.at[1, pl.ds(h1, h1)], rv1c.at[1]),
                to_grid(1, v1a.at[1, pl.ds(own[1], h1)], rv1c.at[0]),
            ]
            start(items)
            finish(items)

            def take0(i, size):
                v0a[pl.ds(i, size)] = rv0[0, pl.ds(i, size)]
                v0a[pl.ds(h0 + n0 + i, size)] = rv0[1, pl.ds(i, size)]
            blocks(0, h0, 4, take0)
            v1a[1, pl.ds(0, h1)] = rv1c[0]
            v1a[1, pl.ds(h1 + own[1], h1)] = rv1c[1]

    half = corr.shape[1] // 2
    first = counter[0]

    def corr_copy(g):
        base = pl.multiple_of(g * SUB, SUB)
        there = pl.multiple_of((1 - samp) * half, LANE)
        return pltpu.make_async_remote_copy(
            src_ref=corr.at[pl.ds(base, SUB), pl.ds(there, half)], dst_ref=rcorr.at[pl.ds(base, SUB)],
            send_sem=send_sem.at[first + g], recv_sem=recv_sem.at[first + g],
            device_id={"samp": 1 - samp}, device_id_type=pl.DeviceIdType.MESH)

    v1a = lev[1]["va"]

    def emit(g, carry):
        base = pl.multiple_of(g * SUB, SUB)
        y = [None] * tiles
        cs = [v1a[1, H[1] + g * (SUB // 2) + r] for r in range(SUB // 2)]
        for p in range(2):
            z = [v0a[h0 + base + r, p] - cs[r // 2] for r in range(SUB)]
            y[p::2] = swap_bits(z, 0, 3)
        y = swap_bits(y, 1, lane_bits)
        for t in range(tiles):
            corr[pl.ds(base, SUB), t * LANE:(t + 1) * LANE] = y[t]
        corr_copy(g).start()
        return carry
    lax.fori_loop(0, gn, emit, 0)

    def combine(g, carry):
        base = pl.multiple_of(g * SUB, SUB)
        corr_copy(g).wait()
        here = pl.multiple_of(samp * half, LANE)
        a = corr[pl.ds(base, SUB), pl.ds(here, half)]
        b = rcorr[pl.ds(base, SUB)]
        m = (a + b) / 2.0
        mean[pl.ds(base, SUB)] = m
        var[pl.ds(base, SUB)] = a * a + b * b - 2.0 * m * m
        return carry
    lax.fori_loop(0, gn, combine, 0)


NAMES = ("c", "nf", "w", "e", "d", "di", "b", "va", "vb")


def entry(grid_count, own, *refs):
    refs = list(refs)
    head, rest = refs[:17], refs[17:]
    lev = {}
    for level in range(1, 5):
        lev[level] = dict(zip(NAMES, rest[:len(NAMES)]))
        rest = rest[len(NAMES):]
    kernel(grid_count, own, *head, lev, *rest)


def local(grid_count, log_coef, source):
    _, n0, cols = log_coef.shape
    own = tuple(n0 >> level for level in range(5))
    assert cols == 2 * SUB * LANE and own[4] * 2 == SUB

    def vm(*shape):
        return pltpu.VMEM(shape + (SUB, LANE), F32)

    t0 = n0 + 2 * HALO[0]
    scratch = [pltpu.VMEM((t0, cols), F32)] * 2
    scratch += [vm(t0, 2)] * 5 + [vm(t0)] * 3 + [vm(t0, 2)] * 2
    for level in range(1, 5):
        t = own[level] + 2 * HALO[level]
        scratch += [vm(t)] * 6 + [vm(2, t)] * 3
    copies = 14 + CYCLES * 8 + n0 // SUB
    scratch += [
        vm(2, HALO[2]), vm(4, own[3]), vm(CYCLES, 2, 2, 5), vm(CYCLES, 2, 2, 3), vm(CYCLES, 4, 2, own[3]),
        vm(2, HALO[0], 2), vm(2, HALO[1]), pltpu.VMEM((n0, cols // 2), F32),
        pltpu.SemaphoreType.DMA((copies,)), pltpu.SemaphoreType.DMA((copies,)), pltpu.SemaphoreType.DMA((2,)),
    ]
    out = [jax.ShapeDtypeStruct((n0, cols), F32)] + [jax.ShapeDtypeStruct((n0, cols // 2), F32)] * 2
    corr, mean, var = pl.pallas_call(
        functools.partial(entry, grid_count, own),
        out_shape=out,
        in_specs=[pl.BlockSpec(memory_space=pl.ANY)] * 2,
        out_specs=[pl.BlockSpec(memory_space=pltpu.VMEM)] * 3,
        scratch_shapes=scratch,
        compiler_params=pltpu.CompilerParams(
            collective_id=0, has_side_effects=True, vmem_limit_bytes=48 * 1024 * 1024),
    )(log_coef, source)
    return corr[None], mean, var


def solution(mesh):
    spec = P("samp", "grid", None)
    return jax.shard_map(
        functools.partial(local, mesh.shape["grid"]), mesh=mesh, in_specs=(spec, spec),
        out_specs=(spec, P("grid", "samp"), P("grid", "samp")), check_vma=False)
```

time: 1260 us -> 114 us (0.09); the launches traced: 1240 us -> 114 us
  local copies, waits for them, and re-layouts: 475 us -> 4.28 us
  starting transfers between devices: 377 us -> 0 us
  other arithmetic: 242 us -> 0 us
  waiting for transfers between devices: 128 us -> 0 us
  Pallas kernels: 0 us -> 109 us
  between operations: 17.9 us -> 0.65 us
    ppermute x118 -> x0, starting transfers between devices: 376 us -> none  [the longest x59 242 us: extended_2(): after = lax.ppermute(initial, axis, down)]
    reshape x52 -> x0, local copies, waits for them, and re-layouts: 198 us -> none  [the longest x14 140 us: quad_sum(): values.reshape(row_count // 2, 2, col_count // 2, 2)]
    pallas_call x0 -> x1, Pallas kernels: none -> 109 us  [local(): pl.pallas_call(functools.partial(entry, grid_count, own), out_shape=out,...]
    reduce_sum x19 -> x0, other arithmetic: 99.1 us -> none  [the longest x15 78.2 us: quad_sum(): jnp.sum(values.reshape(row_count // 2, 2, col_count // 2, 2), axis=(1, 3))]
    slice x179 -> x0, local copies, waits for them, and re-layouts: 85.5 us -> none  [the longest x63 36.5 us: extended_2(): last = lax.slice_in_dim(value, length - width, length, axis=dim)]
    reduce_scatter x2 -> x0, waiting for transfers between devices: 66.2 us -> none  [the longest x1 54.3 us: local(): lax.psum_scatter(correction * correction, 'samp', scatter_dimension=1, ti...]
    ppermute x118 -> x0, waiting for transfers between devices: 60.7 us -> none  [the longest x59 56.8 us: extended_2(): before = lax.ppermute(last, axis, up)]
    another operation x13 -> x0, local copies, waits for them, and re-layouts: 47.1 us -> none  [the longest x1 36.9 us: quad_sum(): values.reshape(row_count // 2, 2, col_count // 2, 2)]
  transfers between devices with their start and end apart: 120 -> 0, of which waited for: 31 -> 0; matrix products, arithmetic and copies ran while one was open for 30% -> 0% of each run, Pallas kernels for 0% -> 0%
where the time goes in v1:
time: 114 us
  Pallas kernels  109 us (96%)
  local copies, waits for them, and re-layouts  4.28 us (4%)
    pallas_call x1, Pallas kernels, local(): pl.pallas_call(functools.partial(entry, grid_count, own), out_shape=out,...  109 us
    unnamed x7, local copies, waits for them, and re-layouts  4.28 us

profile of v1, /device:TPU:17, one launch (start us, length us, event | category | flops | bytes accessed | tf_op | source)
XLA Modules:
  0.0 114.0 jit_solution(11356555812783877264)
XLA Ops:
  0.6 0.0 copy-start
  0.6 1.0 copy-done
  1.7 0.0 copy-start.1
  1.7 1.0 copy-done.1
  2.7 109.1 %shard_map.49 = (f32[64,2048]{1,0:T(8,128)S(1)}, f32[64,1024]{1,0:T(8,128)S(1)}, f32[64,1024]{1,0:T(8,128)S(1)}) custom-call(f32[1,64,2048]{2,1,0:T(8,128)S(1)} %copy-done, f32[1,64,2048]{2,1,0:T(8,128)S(1)} %copy-done.1), custom_call_target="tpu_custom_call" | custom-call | tf_op jit(solution)/shard_map/pallas_call | solution.py:572
  111.8 0.8 copy.8
  112.6 0.7 copy.9
  113.3 0.7 copy.10
Async XLA Ops:
  0.6 1.0 copy-start
  1.7 1.0 copy-start.1

commit v2 on v1

v2 whole, which is shorter than its diff:
```python
import functools

import jax
import jax.numpy as jnp
from jax import lax
from jax.experimental import pallas as pl
from jax.experimental.pallas import tpu as pltpu
from jax.sharding import PartitionSpec as P

CYCLES = 2
LEVELS = 5
SUB = 8
LANE = 128
PAD = 8
HALO = (8, 4, 8, 16, 8)
ROLLED = (True, True, False, False, False)
F32 = jnp.float32


def harmonic(a, b):
    return 2.0 * a * b / (a + b)


def iota(axis):
    return lax.broadcasted_iota(jnp.int32, (SUB, LANE), axis)


def roll(x, shift, axis):
    return pltpu.roll(x, shift % x.shape[axis], axis)


def q_next(x):
    return jnp.where(iota(1) < 112, roll(x, -16, 1), roll(x, -17, 1))


def q_prev(x):
    return jnp.where(iota(1) >= 16, roll(x, 16, 1), roll(x, 17, 1))


def swap_bits(tiles, count):
    tiles = list(tiles)
    for k in range(count):
        w = 1 << k
        bit = (iota(1) // w) % 2 == 1
        for t in range(len(tiles)):
            if t & w == 0:
                a, b = tiles[t], tiles[t | w]
                tiles[t] = jnp.where(bit, roll(b, w, 1), a)
                tiles[t | w] = jnp.where(bit, b, roll(a, -w, 1))
    return tiles


def kernel(grid_count, own, rows, lc_hbm, src_hbm, corr, mean, var, rawc, raws, lev, rc2, rc3, sb1, rv1, rb2, rb3, rv0,
           sc1, rv1c, rcorr, send_sem, recv_sem, load_sem):
    me = lax.axis_index("grid")
    samp = lax.axis_index("samp")
    n0 = own[0]
    counter = [0]
    planes = [lev[level]["c"].shape[0] for level in range(LEVELS)]
    H = HALO
    h0 = H[0]

    def rd(i):
        return pl.ds(PAD + i, SUB)

    def groups(level, body, lo=0, hi=None):
        hi = rows[level] // SUB if hi is None else hi
        if ROLLED[level]:
            def step(g, carry):
                body(pl.multiple_of(g * SUB, SUB))
                return carry
            lax.fori_loop(lo, hi, step, 0)
        else:
            for g in range(lo, hi):
                body(g * SUB)

    def to_grid(dist, src, dst):
        k = counter[0]
        counter[0] += 1
        target = me + dist
        copy = pltpu.make_async_remote_copy(
            src_ref=src, dst_ref=dst, send_sem=send_sem.at[k], recv_sem=recv_sem.at[k],
            device_id={"grid": target}, device_id_type=pl.DeviceIdType.MESH)
        sends = target >= 0 if dist < 0 else target < grid_count
        source = me - dist
        gets = source < grid_count if dist < 0 else source >= 0
        return copy, sends, gets

    def start(items):
        for copy, sends, gets in items:
            @pl.when(sends)
            def _():
                copy.start()

    def finish(items):
        for copy, sends, gets in items:
            @pl.when(sends)
            def _():
                copy.wait_send()

            @pl.when(gets)
            def _():
                copy.wait_recv()

    load_c = pltpu.make_async_copy(lc_hbm.at[0], rawc.at[pl.ds(h0, n0)], load_sem.at[0])
    load_s = pltpu.make_async_copy(src_hbm.at[0], raws.at[pl.ds(h0, n0)], load_sem.at[1])
    load_c.start()
    load_s.start()

    edge = 2
    @pl.when(jnp.logical_or(me < edge, me >= grid_count - edge))
    def _():
        @pl.when(me == 0)
        def _():
            rawc[pl.ds(0, h0)] = jnp.zeros((h0, rawc.shape[1]), F32)
            raws[pl.ds(0, h0)] = jnp.zeros((h0, rawc.shape[1]), F32)

        @pl.when(me == grid_count - 1)
        def _():
            rawc[pl.ds(h0 + n0, h0)] = jnp.zeros((h0, rawc.shape[1]), F32)
            raws[pl.ds(h0 + n0, h0)] = jnp.zeros((h0, rawc.shape[1]), F32)

        for ref in (rc2, rc3):
            for i in range(ref.shape[0]):
                ref[i] = jnp.ones(ref.shape[1:], F32)
        for ref in (rv1, rb2, rb3, rv0, rv1c):
            for i in range(ref.shape[0]):
                ref[i] = jnp.zeros(ref.shape[1:], F32)

    barrier = pltpu.get_barrier_semaphore()
    for dist in (-2, -1, 1, 2):
        inside = me + dist >= 0 if dist < 0 else me + dist < grid_count

        @pl.when(inside)
        def _():
            pl.semaphore_signal(barrier, inc=1, device_id={"grid": me + dist}, device_id_type=pl.DeviceIdType.MESH)
    pl.semaphore_signal(barrier, inc=1, device_id={"samp": 1 - samp}, device_id_type=pl.DeviceIdType.MESH)
    below = jnp.minimum(me, 2)
    above = jnp.minimum(grid_count - 1 - me, 2)
    pl.semaphore_wait(barrier, 1 + below + above)

    raw_items = []
    for hbm, raw in ((lc_hbm, rawc), (src_hbm, raws)):
        raw_items.append(to_grid(-1, hbm.at[0, pl.ds(0, h0)], raw.at[pl.ds(h0 + n0, h0)]))
        raw_items.append(to_grid(1, hbm.at[0, pl.ds(n0 - h0, h0)], raw.at[pl.ds(0, h0)]))
    start(raw_items)

    tiles = rawc.shape[1] // LANE
    lane_bits = tiles.bit_length() - 1

    def split(raw, out, fn, lo, hi):
        def step(g, carry):
            base = pl.multiple_of(g * SUB, SUB)
            y = swap_bits([raw[pl.ds(base, SUB), t * LANE:(t + 1) * LANE] for t in range(tiles)], lane_bits)
            for r in range(tiles):
                out[r, rd(base)] = fn(y[r])
            return carry
        lax.fori_loop(lo, hi, step, 0)

    def same(x):
        return x

    def children(level, j):
        return 2 * (j - H[level]) + H[level - 1]

    def gather_pairs(level, out, starts, scale=None):
        t = lev[level - 1]["t"]
        for k in range(planes[level]):
            for j in starts:
                first = PAD + children(level, j)
                x = t[k, pl.ds(first, SUB, stride=2)] + t[k, pl.ds(first + 1, SUB, stride=2)]
                out[k, rd(j)] = x if scale is None else scale * x

    def reduce_field(level, field, out, starts, lo, hi, scale=None):
        t = lev[level - 1]["t"]

        def body(i):
            for k in range(planes[level]):
                t[k, rd(i)] = field[2 * k, rd(i)] + field[2 * k + 1, rd(i)]
        groups(level - 1, body, lo, hi)
        gather_pairs(level, out, starts, scale)

    def own_starts(level):
        return range(H[level], H[level] + own[level], SUB)

    def all_starts(level):
        return range(0, rows[level], SUB)

    gh, gn = h0 // SUB, n0 // SUB
    c0, b0 = lev[0]["c"], lev[0]["b"].at[0]
    load_c.wait()
    split(rawc, c0, jnp.exp, gh, gh + gn)
    reduce_field(1, c0, lev[1]["c"], own_starts(1), gh, gh + gn, 0.25)
    reduce_field(2, lev[1]["c"], lev[2]["c"], own_starts(2), 0, None, 0.25)
    reduce_field(3, lev[2]["c"], lev[3]["c"], own_starts(3), 1, 3, 0.25)
    c2, c3 = lev[2]["c"], lev[3]["c"]

    def edges(ref, level):
        at = PAD + H[level]
        return pl.ds(at, SUB), pl.ds(at + own[level] - SUB, SUB)

    top2, bottom2 = edges(c2, 2)
    mine3 = pl.ds(PAD + H[3], own[3])
    coef_items = [
        to_grid(-1, c2.at[:, top2], rc2.at[1]),
        to_grid(1, c2.at[:, bottom2], rc2.at[0]),
        to_grid(-1, c3.at[:, mine3], rc3.at[2]),
        to_grid(-2, c3.at[:, mine3], rc3.at[3]),
        to_grid(1, c3.at[:, mine3], rc3.at[1]),
        to_grid(2, c3.at[:, mine3], rc3.at[0]),
    ]
    start(coef_items)
    load_s.wait()
    split(raws, b0, same, gh, gh + gn)
    finish(raw_items)
    for raw, out, fn in ((rawc, c0, jnp.exp), (raws, b0, same)):
        split(raw, out, fn, 0, gh)
        split(raw, out, fn, gh + gn, gh + gn + gh)
    reduce_field(1, c0, lev[1]["c"], all_starts(1), 0, None, 0.25)

    def weights(level):
        L = lev[level]
        R = planes[level]
        c = L["c"]
        first = H[level] - me * own[level]
        end = H[level] + (grid_count - me) * own[level]

        def vertical(i):
            at = iota(0) + i
            for r in range(R):
                a, b = c[r, rd(i - 1)], c[r, rd(i)]
                L["nf"][r, rd(i)] = harmonic(jnp.where(at == first, b, a), jnp.where(at == end, a, b))
        groups(level, vertical)

        def body(i):
            at = iota(0) + i
            inside = jnp.logical_and(at >= first, at < end)
            u = [c[r, rd(i)] for r in range(R)]
            we, ee = iota(1) == 0, iota(1) == LANE - 1
            faces = [harmonic(jnp.where(we, u[0], q_prev(u[-1])), u[0])]
            faces += [harmonic(u[r - 1], u[r]) for r in range(1, R)]
            faces += [harmonic(u[-1], jnp.where(ee, u[-1], q_next(u[0])))]
            for r in range(R):
                d = faces[r] + faces[r + 1] + L["nf"][r, rd(i)] + L["nf"][r, rd(i + 1)]
                L["d"][r, rd(i)] = d
                L["di"][r, rd(i)] = jnp.where(inside, 0.8 / d, 0.0)
            for r in range(R + 1):
                edge = we if r == 0 else ee
                L["hf"][r, rd(i)] = jnp.where(edge, 0.0, faces[r]) if r in (0, R) else faces[r]
        groups(level, body)

    def around(level, v, i, out):
        L = lev[level]
        R = planes[level]
        count = v.shape[0]
        prev, here, first, west = [], [], [], []
        for pr in range(count):
            first.append(v[pr, 0, rd(i)])
            west.append(q_prev(v[pr, R - 1, rd(i)]))
        here = list(first)
        for r in range(R):
            wf, ef = L["hf"][r, rd(i)], L["hf"][r + 1, rd(i)]
            nf, sf = L["nf"][r, rd(i)], L["nf"][r, rd(i + 1)]
            for pr in range(count):
                after = v[pr, r + 1, rd(i)] if r + 1 < R else None
                east = after if r + 1 < R else q_next(first[pr])
                total = (wf * west[pr] + ef * east) + (nf * v[pr, r, rd(i - 1)] + sf * v[pr, r, rd(i + 1)])
                out(pr, r, here[pr], total)
                west[pr], here[pr] = here[pr], after

    def sweep(level, src, dst, lo=0, hi=None):
        L = lev[level]

        def body(i):
            def out(pr, r, u, total):
                dst[pr, r, rd(i)] = 0.2 * u + L["di"][r, rd(i)] * (L["b"][pr, r, rd(i)] + total)
            around(level, src, i, out)
        groups(level, body, lo, hi)

    def first_sweep(level, dst):
        L = lev[level]

        def body(i):
            for r in range(planes[level]):
                for pr in range(dst.shape[0]):
                    dst[pr, r, rd(i)] = L["di"][r, rd(i)] * L["b"][pr, r, rd(i)]
        groups(level, body)

    def restrict(level, v, starts):
        L = lev[level]
        t2 = (L["t"], L["t2"]) if level else (L["t"],)

        def body(i):
            held = {}

            def out(pr, r, u, total):
                x = L["b"][pr, r, rd(i)] - L["d"][r, rd(i)] * u + total
                if r % 2 == 0:
                    held[pr] = x
                else:
                    t2[pr][r // 2, rd(i)] = held[pr] + x
            around(level, v, i, out)
        groups(level, body)
        for pr in range(v.shape[0]):
            out = lev[level + 1]["b"]
            for k in range(planes[level + 1]):
                for j in starts:
                    first = PAD + children(level + 1, j)
                    out[pr, k, rd(j)] = (t2[pr][k, pl.ds(first, SUB, stride=2)]
                                         + t2[pr][k, pl.ds(first + 1, SUB, stride=2)])

    def correct(level, v, e, starts, pairs, sign=1.0):
        def body(k):
            for pr, pe in pairs:
                for j in starts:
                    x = e[pe, k, rd(j)]
                    first = PAD + children(level + 1, j)
                    for r in range(2):
                        for h in range(2):
                            at = pl.ds(first + h, SUB, stride=2)
                            y = v[pr, 2 * k + r, at]
                            v[pr, 2 * k + r, at] = y + x if sign > 0 else y - x
        if ROLLED[level]:
            lax.fori_loop(0, planes[level + 1], lambda k, c: (body(k), c)[1], 0)
        else:
            for k in range(planes[level + 1]):
                body(k)

    weights(0)
    weights(1)
    b1, v1a, v1b = lev[1]["b"], lev[1]["va"], lev[1]["vb"]
    v0a, v0b = lev[0]["va"], lev[0]["vb"]
    reduce_field(1, b0, b1.at[1], all_starts(1), 0, None)
    h1, n1 = H[1], own[1]
    R1 = planes[1]
    both = ((0, 0), (1, 1))

    for cycle in range(CYCLES):
        if cycle == 0:
            first_sweep(0, v0b)
        else:
            sweep(0, v0a, v0b)
        sweep(0, v0b, v0a)
        restrict(0, v0a, all_starts(1))
        if cycle == 0:
            first_sweep(1, v1b)
        else:
            def clear(i):
                for r in range(R1):
                    v1a[0, r, rd(i)] = jnp.zeros((SUB, LANE), F32)
            groups(1, clear)
            sweep(1, v1a, v1b)
        sweep(1, v1b, v1a)
        restrict(1, v1a, own_starts(2))
        b2 = lev[2]["b"]
        for pr in range(2):
            for r in range(R1):
                sb1[cycle, 0, pr, r] = v1a[pr, r, rd(h1)]
                sb1[cycle, 1, pr, r] = v1a[pr, r, rd(h1 + n1 - SUB)]
        items = [
            to_grid(-1, b2.at[:, :, top2], rb2.at[cycle, 1]),
            to_grid(1, b2.at[:, :, bottom2], rb2.at[cycle, 0]),
            to_grid(-1, sb1.at[cycle, 0], rv1.at[cycle, 1]),
            to_grid(1, sb1.at[cycle, 1], rv1.at[cycle, 0]),
        ]
        start(items)
        if cycle == 0:
            finish(coef_items)
            for r in range(planes[2]):
                c2[r, rd(0)] = rc2[0, r]
                c2[r, rd(H[2] + own[2])] = rc2[1, r]
            for s, at in enumerate((0, SUB, H[3] + SUB, H[3] + 2 * SUB)):
                for r in range(planes[3]):
                    c3[r, rd(at)] = rc3[s, r]
            reduce_field(4, c3, lev[4]["c"], all_starts(4), 0, None, 0.25)
            for level in (2, 3, 4):
                weights(level)
        finish(items)
        for pr in range(2):
            for r in range(planes[2]):
                b2[pr, r, rd(0)] = rb2[cycle, 0, pr, r]
                b2[pr, r, rd(H[2] + own[2])] = rb2[cycle, 1, pr, r]
            for r in range(R1):
                v1a[pr, r, pl.ds(PAD, h1)] = rv1[cycle, 0, pr, r, SUB - h1:, :]
                v1a[pr, r, pl.ds(PAD + h1 + n1, h1)] = rv1[cycle, 1, pr, r, :h1, :]
        v2a, v2b = lev[2]["va"], lev[2]["vb"]
        first_sweep(2, v2b)
        sweep(2, v2b, v2a)
        restrict(2, v2a, own_starts(3))
        b3 = lev[3]["b"]
        mine = b3.at[:, :, mine3]
        items = [
            to_grid(-1, mine, rb3.at[cycle, 2]),
            to_grid(-2, mine, rb3.at[cycle, 3]),
            to_grid(1, mine, rb3.at[cycle, 1]),
            to_grid(2, mine, rb3.at[cycle, 0]),
        ]
        start(items)
        finish(items)
        for s, at in enumerate((0, SUB, H[3] + SUB, H[3] + 2 * SUB)):
            for pr in range(2):
                for r in range(planes[3]):
                    b3[pr, r, rd(at)] = rb3[cycle, s, pr, r]
        v3a, v3b = lev[3]["va"], lev[3]["vb"]
        v4a, v4b = lev[4]["va"], lev[4]["vb"]
        first_sweep(3, v3b)
        sweep(3, v3b, v3a)
        restrict(3, v3a, all_starts(4))
        first_sweep(4, v4b)
        sweep(4, v4b, v4a)
        sweep(4, v4a, v4b)
        sweep(4, v4b, v4a)
        correct(3, v3a, v4a, all_starts(4), both)
        sweep(3, v3a, v3b)
        sweep(3, v3b, v3a)
        correct(2, v2a, v3a, (H[3] - 4, H[3] + 4), both)
        sweep(2, v2a, v2b)
        sweep(2, v2b, v2a)
        correct(1, v1a, v2a, (H[2] - 2, H[2] + 6, H[2] + 14), both)
        sweep(1, v1a, v1b)
        sweep(1, v1b, v1a)
        correct(0, v0a, v1a, all_starts(1), ((0, 0),))
        sweep(0, v0a, v0b)
        sweep(0, v0b, v0a, gh, gh + gn)
        if cycle < CYCLES - 1:
            for r in range(R1):
                sc1[0, r] = v1a[1, r, rd(h1)]
                sc1[1, r] = v1a[1, r, rd(h1 + n1 - SUB)]
            top0, bottom0 = edges(v0a, 0)
            items = [
                to_grid(-1, v0a.at[0, :, top0], rv0.at[1]),
                to_grid(1, v0a.at[0, :, bottom0], rv0.at[0]),
                to_grid(-1, sc1.at[0], rv1c.at[1]),
                to_grid(1, sc1.at[1], rv1c.at[0]),
            ]
            start(items)
            finish(items)
            for r in range(planes[0]):
                v0a[0, r, rd(0)] = rv0[0, r]
                v0a[0, r, rd(h0 + n0)] = rv0[1, r]
            for r in range(R1):
                v1a[1, r, pl.ds(PAD, h1)] = rv1c[0, r, SUB - h1:, :]
                v1a[1, r, pl.ds(PAD + h1 + n1, h1)] = rv1c[1, r, :h1, :]
    correct(0, v0a, v1a, own_starts(1), ((0, 1),), -1.0)

    half = corr.shape[1] // 2
    first = counter[0]

    def corr_copy(g):
        base = pl.multiple_of(g * SUB, SUB)
        there = pl.multiple_of((1 - samp) * half, LANE)
        return pltpu.make_async_remote_copy(
            src_ref=corr.at[pl.ds(base, SUB), pl.ds(there, half)], dst_ref=rcorr.at[pl.ds(base, SUB)],
            send_sem=send_sem.at[first + g], recv_sem=recv_sem.at[first + g],
            device_id={"samp": 1 - samp}, device_id_type=pl.DeviceIdType.MESH)

    def emit(g, carry):
        base = pl.multiple_of(g * SUB, SUB)
        y = swap_bits([v0a[0, r, rd(h0 + base)] for r in range(tiles)], lane_bits)
        for t in range(tiles):
            corr[pl.ds(base, SUB), t * LANE:(t + 1) * LANE] = y[t]
        corr_copy(g).start()
        return carry
    lax.fori_loop(0, gn, emit, 0)

    def combine(g, carry):
        base = pl.multiple_of(g * SUB, SUB)
        corr_copy(g).wait()
        here = pl.multiple_of(samp * half, LANE)
        a = corr[pl.ds(base, SUB), pl.ds(here, half)]
        b = rcorr[pl.ds(base, SUB)]
        m = (a + b) / 2.0
        mean[pl.ds(base, SUB)] = m
        var[pl.ds(base, SUB)] = a * a + b * b - 2.0 * m * m
        return carry
    lax.fori_loop(0, gn, combine, 0)


NAMES = ("c", "nf", "hf", "d", "di", "t", "t2", "b", "va", "vb")


def entry(grid_count, own, rows, *refs):
    refs = list(refs)
    head, rest = refs[:7], refs[7:]
    lev = {}
    for level in range(LEVELS):
        lev[level] = dict(zip(NAMES, rest[:len(NAMES)]))
        rest = rest[len(NAMES):]
    kernel(grid_count, own, rows, *head, lev, *rest)


def local(grid_count, log_coef, source):
    _, n0, cols = log_coef.shape
    own = tuple(n0 >> level for level in range(LEVELS))
    rows = tuple(-(-(own[level] + 2 * HALO[level]) // SUB) * SUB for level in range(LEVELS))
    assert cols == LANE << (LEVELS - 1) and own[LEVELS - 1] * 2 == SUB

    def vm(*shape):
        return pltpu.VMEM(shape + (LANE,), F32)

    scratch = [pltpu.VMEM((n0 + 2 * HALO[0], cols), F32)] * 2
    R = [cols // LANE >> level for level in range(LEVELS)]
    for level in range(LEVELS):
        t, r, count = rows[level] + 2 * PAD, R[level], 2 if level else 1
        scratch += [vm(r, t), vm(r, t), vm(r + 1, t), vm(r, t), vm(r, t)]
        scratch += [vm(max(r // 2, 1), t)] * 2 + [vm(count, r, t)] * 3
    copies = 14 + CYCLES * 8 + n0 // SUB
    scratch += [
        vm(2, R[2], SUB), vm(4, R[3], SUB), vm(CYCLES, 2, 2, R[1], SUB), vm(CYCLES, 2, 2, R[1], SUB),
        vm(CYCLES, 2, 2, R[2], SUB), vm(CYCLES, 4, 2, R[3], SUB), vm(2, R[0], SUB), vm(2, R[1], SUB),
        vm(2, R[1], SUB), pltpu.VMEM((n0, cols // 2), F32),
        pltpu.SemaphoreType.DMA((copies,)), pltpu.SemaphoreType.DMA((copies,)), pltpu.SemaphoreType.DMA((2,)),
    ]
    out = [jax.ShapeDtypeStruct((n0, cols), F32)] + [jax.ShapeDtypeStruct((n0, cols // 2), F32)] * 2
    corr, mean, var = pl.pallas_call(
        functools.partial(entry, grid_count, own, rows),
        out_shape=out,
        in_specs=[pl.BlockSpec(memory_space=pl.ANY)] * 2,
        out_specs=[pl.BlockSpec(memory_space=pltpu.VMEM)] * 3,
        scratch_shapes=scratch,
        compiler_params=pltpu.CompilerParams(
            collective_id=0, has_side_effects=True, vmem_limit_bytes=48 * 1024 * 1024),
    )(log_coef, source)
    return corr[None], mean, var


def solution(mesh):
    spec = P("samp", "grid", None)
    return jax.shard_map(
        functools.partial(local, mesh.shape["grid"]), mesh=mesh, in_specs=(spec, spec),
        out_specs=(spec, P("grid", "samp"), P("grid", "samp")), check_vma=False)
```

time: 114 us -> 58 us (0.51)
  Pallas kernels: 109 us -> 52.9 us
    pallas_call x1, Pallas kernels: 109 us -> 52.9 us  [local(): pl.pallas_call(functools.partial(entry, grid_count, own, rows), out_shape...]
where the time goes in v2:
time: 58 us; the launch traced here: 57.8 us
  Pallas kernels  52.9 us (91%)
  local copies, waits for them, and re-layouts  4.28 us (7%)
  between operations  0.65 us (1%)
    pallas_call x1, Pallas kernels, local(): pl.pallas_call(functools.partial(entry, grid_count, own, rows), out_shape...  52.9 us
    unnamed x7, local copies, waits for them, and re-layouts  4.28 us

profile of v2, /device:TPU:17, one launch (start us, length us, event | category | flops | bytes accessed | tf_op | source)
XLA Modules:
  0.0 57.8 jit_solution(12887242899738506393)
XLA Ops:
  0.6 0.0 copy-start
  0.6 1.0 %copy-done = f32[1,64,2048]{2,1,0:T(8,128)S(1)} copy-done((f32[1,64,2048]{2,1,0:T(8,128)S(1)}, f32[1,64,2048]{2,1,0:T(8,128)}, u32[]{:S(2)}) %copy-start) | copy-done | bytes 524312
  1.7 0.0 copy-start.1
  1.7 1.0 %copy-done.1 = f32[1,64,2048]{2,1,0:T(8,128)S(1)} copy-done((f32[1,64,2048]{2,1,0:T(8,128)S(1)}, f32[1,64,2048]{2,1,0:T(8,128)}, u32[]{:S(2)}) %copy-start.1) | copy-done | bytes 524312
  2.7 52.9 %shard_map.49 = (f32[64,2048]{1,0:T(8,128)S(1)}, f32[64,1024]{1,0:T(8,128)S(1)}, f32[64,1024]{1,0:T(8,128)S(1)}) custom-call(f32[1,64,2048]{2,1,0:T(8,128)S(1)} %copy-done, f32[1,64,2048]{2,1,0:T(8,128)S(1)} %copy-done.1), custom_call_target="tpu_custom_call" | custom-call | tf_op jit(solution)/shard_map/pallas_call | solution.py:515
  55.6 0.8 %copy.8 = f32[1,64,2048]{2,1,0:T(8,128)} copy(f32[1,64,2048]{2,1,0:T(8,128)S(1)} %bitcast.1) | data formatting | bytes 1048576
  56.4 0.7 %copy.9 = f32[64,1024]{1,0:T(8,128)} copy(f32[64,1024]{1,0:T(8,128)S(1)} %get-tuple-element.13) | data formatting | bytes 524288
  57.1 0.7 %copy.10 = f32[64,1024]{1,0:T(8,128)} copy(f32[64,1024]{1,0:T(8,128)S(1)} %get-tuple-element.14) | data formatting | bytes 524288
Async XLA Ops:
  0.6 1.0 %copy-start = (f32[1,64,2048]{2,1,0:T(8,128)S(1)}, f32[1,64,2048]{2,1,0:T(8,128)}, u32[]{:S(2)}) copy-start(f32[1,64,2048]{2,1,0:T(8,128)} %refs_0_.1) | copy-start | bytes 1572868
  1.7 1.0 %copy-start.1 = (f32[1,64,2048]{2,1,0:T(8,128)S(1)}, f32[1,64,2048]{2,1,0:T(8,128)}, u32[]{:S(2)}) copy-start(f32[1,64,2048]{2,1,0:T(8,128)} %refs_1_.1) | copy-start | bytes 1572868

commit v3 on v2

--- a/solution.py
+++ b/solution.py
@@ -14,6 +14,7 @@
 PAD = 8
 HALO = (8, 4, 8, 16, 8)
 ROLLED = (True, True, False, False, False)
+BATCH = 16
 F32 = jnp.float32
 
 
@@ -63,16 +64,25 @@
     def rd(i):
         return pl.ds(PAD + i, SUB)
 
+    def put(stores):
+        for ref, at, value in stores or ():
+            ref[at] = value
+
     def groups(level, body, lo=0, hi=None):
         hi = rows[level] // SUB if hi is None else hi
         if ROLLED[level]:
             def step(g, carry):
-                body(pl.multiple_of(g * SUB, SUB))
+                put(body(pl.multiple_of(g * SUB, SUB)))
                 return carry
             lax.fori_loop(lo, hi, step, 0)
         else:
+            held = []
             for g in range(lo, hi):
-                body(g * SUB)
+                held += body(g * SUB) or []
+                if len(held) >= BATCH:
+                    put(held)
+                    held = []
+            put(held)
 
     def to_grid(dist, src, dst):
         k = counter[0]
@@ -175,8 +185,7 @@
         t = lev[level - 1]["t"]
 
         def body(i):
-            for k in range(planes[level]):
-                t[k, rd(i)] = field[2 * k, rd(i)] + field[2 * k + 1, rd(i)]
+            return [(t, (k, rd(i)), field[2 * k, rd(i)] + field[2 * k + 1, rd(i)]) for k in range(planes[level])]
         groups(level - 1, body, lo, hi)
         gather_pairs(level, out, starts, scale)
 
@@ -227,9 +236,12 @@
 
         def vertical(i):
             at = iota(0) + i
+            stores = []
             for r in range(R):
                 a, b = c[r, rd(i - 1)], c[r, rd(i)]
-                L["nf"][r, rd(i)] = harmonic(jnp.where(at == first, b, a), jnp.where(at == end, a, b))
+                x = harmonic(jnp.where(at == first, b, a), jnp.where(at == end, a, b))
+                stores.append((L["nf"], (r, rd(i)), x))
+            return stores
         groups(level, vertical)
 
         def body(i):
@@ -272,18 +284,21 @@
         L = lev[level]
 
         def body(i):
+            stores = []
+
             def out(pr, r, u, total):
-                dst[pr, r, rd(i)] = 0.2 * u + L["di"][r, rd(i)] * (L["b"][pr, r, rd(i)] + total)
+                x = 0.2 * u + L["di"][r, rd(i)] * (L["b"][pr, r, rd(i)] + total)
+                stores.append((dst, (pr, r, rd(i)), x))
             around(level, src, i, out)
+            return stores
         groups(level, body, lo, hi)
 
     def first_sweep(level, dst):
         L = lev[level]
 
         def body(i):
-            for r in range(planes[level]):
-                for pr in range(dst.shape[0]):
-                    dst[pr, r, rd(i)] = L["di"][r, rd(i)] * L["b"][pr, r, rd(i)]
+            return [(dst, (pr, r, rd(i)), L["di"][r, rd(i)] * L["b"][pr, r, rd(i)])
+                    for r in range(planes[level]) for pr in range(dst.shape[0])]
         groups(level, body)
 
     def restrict(level, v, starts):
@@ -291,15 +306,16 @@
         t2 = (L["t"], L["t2"]) if level else (L["t"],)
 
         def body(i):
-            held = {}
+            held, stores = {}, []
 
             def out(pr, r, u, total):
                 x = L["b"][pr, r, rd(i)] - L["d"][r, rd(i)] * u + total
                 if r % 2 == 0:
                     held[pr] = x
                 else:
-                    t2[pr][r // 2, rd(i)] = held[pr] + x
+                    stores.append((t2[pr], (r // 2, rd(i)), held[pr] + x))
             around(level, v, i, out)
+            return stores
         groups(level, body)
         for pr in range(v.shape[0]):
             out = lev[level + 1]["b"]
@@ -311,6 +327,7 @@
 
     def correct(level, v, e, starts, pairs, sign=1.0):
         def body(k):
+            stores = []
             for pr, pe in pairs:
                 for j in starts:
                     x = e[pe, k, rd(j)]
@@ -319,7 +336,8 @@
                         for h in range(2):
                             at = pl.ds(first + h, SUB, stride=2)
                             y = v[pr, 2 * k + r, at]
-                            v[pr, 2 * k + r, at] = y + x if sign > 0 else y - x
+                            stores.append((v, (pr, 2 * k + r, at), y + x if sign > 0 else y - x))
+            put(stores)
         if ROLLED[level]:
             lax.fori_loop(0, planes[level + 1], lambda k, c: (body(k), c)[1], 0)
         else:
@@ -339,7 +357,8 @@
         if cycle == 0:
             first_sweep(0, v0b)
         else:
-            sweep(0, v0a, v0b)
+            sweep(0, v0a, v0b, 0, gh + 1)
+            sweep(0, v0a, v0b, gh + gn - 1, None)
         sweep(0, v0b, v0a)
         restrict(0, v0a, all_starts(1))
         if cycle == 0:
@@ -421,8 +440,11 @@
         sweep(1, v1b, v1a)
         correct(0, v0a, v1a, all_starts(1), ((0, 0),))
         sweep(0, v0a, v0b)
-        sweep(0, v0b, v0a, gh, gh + gn)
-        if cycle < CYCLES - 1:
+        if cycle == CYCLES - 1:
+            sweep(0, v0b, v0a, gh, gh + gn)
+        else:
+            sweep(0, v0b, v0a, gh, gh + 1)
+            sweep(0, v0b, v0a, gh + gn - 1, gh + gn)
             for r in range(R1):
                 sc1[0, r] = v1a[1, r, rd(h1)]
                 sc1[1, r] = v1a[1, r, rd(h1 + n1 - SUB)]
@@ -434,6 +456,8 @@
                 to_grid(1, sc1.at[1], rv1c.at[0]),
             ]
             start(items)
+            sweep(0, v0b, v0a, gh + 1, gh + gn - 1)
+            sweep(0, v0a, v0b, gh + 1, gh + gn - 1)
             finish(items)
             for r in range(planes[0]):
                 v0a[0, r, rd(0)] = rv0[0, r]
@@ -502,6 +526,7 @@
     R = [cols // LANE >> level for level in range(LEVELS)]
     for level in range(LEVELS):
         t, r, count = rows[level] + 2 * PAD, R[level], 2 if level else 1
+        t += SUB * (1 - t // SUB % 2)
         scratch += [vm(r, t), vm(r, t), vm(r + 1, t), vm(r, t), vm(r, t)]
         scratch += [vm(max(r // 2, 1), t)] * 2 + [vm(count, r, t)] * 3
     copies = 14 + CYCLES * 8 + n0 // SUB

time: 58 us -> 56.8 us (0.979)
  Pallas kernels: 52.9 us -> 51.7 us
    pallas_call x1, Pallas kernels: 52.9 us -> 51.7 us  [local(): pl.pallas_call(functools.partial(entry, grid_count, own, rows), out_shape...]
where the time goes in v3:
time: 56.8 us; the launch traced here: 56.6 us
  Pallas kernels  51.7 us (91%)
  local copies, waits for them, and re-layouts  4.28 us (8%)
  between operations  0.65 us (1%)
    pallas_call x1, Pallas kernels, local(): pl.pallas_call(functools.partial(entry, grid_count, own, rows), out_shape...  51.7 us
    unnamed x7, local copies, waits for them, and re-layouts  4.28 us

profile of v3, /device:TPU:17, one launch (start us, length us, event | category | flops | bytes accessed | tf_op | source)
XLA Modules:
  0.0 56.6 jit_solution(6502254965367581532)
XLA Ops:
  0.6 0.0 copy-start
  0.6 1.0 %copy-done = f32[1,64,2048]{2,1,0:T(8,128)S(1)} copy-done((f32[1,64,2048]{2,1,0:T(8,128)S(1)}, f32[1,64,2048]{2,1,0:T(8,128)}, u32[]{:S(2)}) %copy-start) | copy-done | bytes 524312
  1.7 0.0 copy-start.1
  1.7 1.0 %copy-done.1 = f32[1,64,2048]{2,1,0:T(8,128)S(1)} copy-done((f32[1,64,2048]{2,1,0:T(8,128)S(1)}, f32[1,64,2048]{2,1,0:T(8,128)}, u32[]{:S(2)}) %copy-start.1) | copy-done | bytes 524312
  2.7 51.7 %shard_map.49 = (f32[64,2048]{1,0:T(8,128)S(1)}, f32[64,1024]{1,0:T(8,128)S(1)}, f32[64,1024]{1,0:T(8,128)S(1)}) custom-call(f32[1,64,2048]{2,1,0:T(8,128)S(1)} %copy-done, f32[1,64,2048]{2,1,0:T(8,128)S(1)} %copy-done.1), custom_call_target="tpu_custom_call" | custom-call | tf_op jit(solution)/shard_map/pallas_call | solution.py:540
  54.4 0.8 %copy.8 = f32[1,64,2048]{2,1,0:T(8,128)} copy(f32[1,64,2048]{2,1,0:T(8,128)S(1)} %bitcast.1) | data formatting | bytes 1048576
  55.2 0.7 %copy.9 = f32[64,1024]{1,0:T(8,128)} copy(f32[64,1024]{1,0:T(8,128)S(1)} %get-tuple-element.13) | data formatting | bytes 524288
  55.9 0.7 %copy.10 = f32[64,1024]{1,0:T(8,128)} copy(f32[64,1024]{1,0:T(8,128)S(1)} %get-tuple-element.14) | data formatting | bytes 524288
Async XLA Ops:
  0.6 1.0 %copy-start = (f32[1,64,2048]{2,1,0:T(8,128)S(1)}, f32[1,64,2048]{2,1,0:T(8,128)}, u32[]{:S(2)}) copy-start(f32[1,64,2048]{2,1,0:T(8,128)} %refs_0_.1) | copy-start | bytes 1572868
  1.7 1.0 %copy-start.1 = (f32[1,64,2048]{2,1,0:T(8,128)S(1)}, f32[1,64,2048]{2,1,0:T(8,128)}, u32[]{:S(2)}) copy-start(f32[1,64,2048]{2,1,0:T(8,128)} %refs_1_.1) | copy-start | bytes 1572868
